TPU v7x, 128 devices: a whole 4x4x4 slice. The times are simulated.
128 devices in a mesh: blk: 8 (over z, core), lat: 16 (over x, y).
Axes of the slice: x: 4, y: 4, z: 4, core: 2. Of those that a mesh axis runs over, the one named last changes fastest.
Arguments:
- ice_area: float32 [5, 12, 512, 8192], P(None, None, 'lat', 'blk'), may hold values from 0.05 to 1
- departure_weights: int32 [9, 512, 8192], P(None, 'lat', 'blk'), may hold values from 0 to 4096, as said below
- weld_rate: float32 [512, 8192], P('lat', 'blk'), may hold values from 0.1 to 1
- ice_cover: int32 [512, 8], P('lat', 'blk'), may hold values from 0 to 1, as said below
- wave_ocean: float32 [128, 25, 128, 256], P(('blk', 'lat')), may hold values from 0.02 to 0.5
- ocean_route: int32 [128, 128], P(('blk', 'lat')), may hold values from 0 to 127, each once within a row
Outputs:
- new_area: float32 [5, 12, 512, 8192], P(None, None, 'lat', 'blk')
Inputs may be any that keep to these rules, and one draw needn't show every extreme that they name: `departure_weights`: the nine weights of a cell sum to 4096; each off-centre weight is below 410. `ice_cover`: each device's count of ice-covered rows is a multiple of 2, from 2 to 32; in every longitude band the 16 devices' counts are 2, 4, ..., 32 in some order, so a band holds exactly 272 ice-covered blocks. `ocean_route`: each row is a permutation: every ocean device sends one wave block to every ice device.
All inputs are finite; a program needn't handle non-finite values.
Results may differ from a plain program's by a relative error of at most 0.0001.
Values sent between devices are 32-bit elements; how exact they have to be, the bound alone decides.
A program may use at most 192 MiB of HBM per device.

v0:
```python
import jax
import jax.numpy as jnp
from jax import lax
from jax.experimental import pallas as pl
from jax.experimental.pallas import tpu as pltpu
from jax.sharding import PartitionSpec as P

NCAT = 5
NFSD = 12
CATS = NCAT * NFSD
FREQ = 25
ROWS = 32
COLS = 1024
GROUPS = ROWS // 8
TILES = COLS // 128
NBLK = 8
NLAT = 16
PEERS = NBLK * NLAT
MESH = pl.DeviceIdType.MESH
FLAT = 2 * PEERS
FRONT_LIMIT = 34 * 1024 * 1024
BACK_LIMIT = 16 * 1024 * 1024


def vmem_spec():
    return pl.BlockSpec(memory_space=pltpu.VMEM)


def any_spec():
    return pl.BlockSpec(memory_space=pltpu.HBM)


def front_kernel(route_hbm, wave_hbm, ice_hbm, shares_hbm, moved_ref, rate_ref,
                 wave_v, sums_v, send_v, mid_v, turn_v, ice_v, shares_v, weights_v,
                 south_v, north_v, got_south, got_north, west_v, east_v, got_west, got_east, corner_v,
                 west_h, east_h, route_v, route_sem, wave_sem, ice_sem, shares_sem,
                 lat_send, lat_recv, blk_send, blk_recv, send_sem, recv_sem):
    f32 = jnp.float32
    b = lax.axis_index("blk")
    l = lax.axis_index("lat")
    east_b = lax.rem(b + 1, NBLK)
    west_b = lax.rem(b + NBLK - 1, NBLK)
    at_north = l == NLAT - 1
    at_south = l == 0
    inner_north = l < NLAT - 1
    inner_south = l > 0
    up = jnp.minimum(l + 1, NLAT - 1)
    down = jnp.maximum(l - 1, 0)

    parts = 4
    share = PEERS // parts
    wave_copies = [
        pltpu.make_async_copy(
            wave_hbm.at[:, pl.ds(share * i, share), :], wave_v.at[:, pl.ds(share * i, share), :], wave_sem.at[i]
        )
        for i in range(parts)
    ]
    ice_copies = {
        (g, j): pltpu.make_async_copy(
            ice_hbm.at[:, pl.ds(8 * g, 8), pl.ds(128 * j, 128)],
            ice_v.at[j, :, pl.ds(8 + 8 * g, 8), :],
            ice_sem.at[g, j],
        )
        for g in range(GROUPS)
        for j in range(TILES)
    }
    shares_copy = pltpu.make_async_copy(shares_hbm, shares_v, shares_sem)
    route_copy = pltpu.make_async_copy(route_hbm, route_v, route_sem)
    for copy in [route_copy] + wave_copies:
        copy.start()
    for g in (0, 3, 1, 2):
        for j in range(TILES):
            ice_copies[g, j].start()
        if g == 3:
            shares_copy.start()

    barrier = pltpu.get_barrier_semaphore()

    def greet(dev):
        pl.semaphore_signal(barrier, inc=1, device_id=dev, device_id_type=MESH)

    for k in range(1, NLAT):
        greet((b, lax.rem(l + k, NLAT)))
    for k in range(1, NBLK):
        greet((lax.rem(b + k, NBLK), l))
    for side in (east_b, west_b):
        greet((side, lax.rem(l + 1, NLAT)))
        greet((side, lax.rem(l + NLAT - 1, NLAT)))

    for j in range(TILES):
        for first in range(0, CATS, 8):
            size = min(8, CATS - first)
            for spot in (7, 8 + ROWS):
                ice_v[j, pl.ds(first, size), spot, :] = jnp.zeros((size, 128), f32)

    for i in range(parts):
        wave_copies[i].wait()

        def rows(block, carry):
            first = pl.multiple_of(share * i + block * 8, 8)
            for half in range(2):
                lanes = pl.ds(128 * half, 128)
                total = wave_v[0, pl.ds(first, 8), lanes]
                for f in range(1, FREQ):
                    total = total + wave_v[f, pl.ds(first, 8), lanes] * (f + 1.0)
                sums_v[half, pl.ds(first, 8), :] = total
            return carry

        lax.fori_loop(0, share // 8, rows, 0)

    route_copy.wait()
    route = route_v[...]
    place = (jnp.bitwise_and(route, NLAT - 1) * NBLK + jnp.right_shift(route, 4)) * 2
    row = lax.broadcasted_iota(jnp.int32, (FLAT, PEERS), 0)
    ordered = jnp.zeros((FLAT, 128), f32)
    for half in range(2):
        chosen = (row == place + half).astype(f32)
        ordered = ordered + jnp.dot(
            chosen, sums_v[half], precision=lax.Precision.HIGHEST, preferred_element_type=f32
        )
    send_v[...] = ordered

    pl.semaphore_wait(barrier, NLAT - 1 + NBLK - 1 + 4)

    def lat_copy(k):
        peer = lax.rem(l + k, NLAT)
        return pltpu.make_async_remote_copy(
            src_ref=send_v.at[pl.ds(pl.multiple_of(16 * peer, 16), 16), :],
            dst_ref=mid_v.at[pl.ds(pl.multiple_of(16 * l, 16), 16), :],
            send_sem=lat_send.at[k], recv_sem=lat_recv.at[k],
            device_id=(b, peer), device_id_type=MESH,
        )

    for k in range(1, NLAT):
        lat_copy(k).start()
    mine = pl.ds(pl.multiple_of(16 * l, 16), 16)
    mid_v[mine, :] = send_v[mine, :]

    def remote(source, target, sent, got, dev):
        return pltpu.make_async_remote_copy(
            src_ref=source, dst_ref=target, send_sem=send_sem.at[sent], recv_sem=recv_sem.at[got],
            device_id=dev, device_id_type=MESH,
        )

    for g, spot, target in ((0, 8, south_v), (3, 7 + ROWS, north_v)):
        for j in range(TILES):
            ice_copies[g, j].wait()
        for first in range(0, CATS, 8):
            size = min(8, CATS - first)
            for j in range(TILES):
                target[pl.ds(first, size), pl.ds(128 * j, 128)] = ice_v[j, pl.ds(first, size), spot, :]

    to_south = remote(south_v, got_north, 6, 6, (b, down))
    to_north = remote(north_v, got_south, 7, 7, (b, up))
    over = remote(north_v, got_north, 10, 6, (NBLK - 1 - b, l))

    @pl.when(inner_south)
    def _():
        to_south.start()

    @pl.when(inner_north)
    def _():
        to_north.start()

    @pl.when(at_north)
    def _():
        over.start()

    lane = lax.broadcasted_iota(jnp.int32, (8, 128), 1)
    for g in (0, 3, 1, 2):
        if g in (1, 2):
            for j in range(TILES):
                ice_copies[g, j].wait()
        for tile, target, edge in ((0, west_v, 0), (TILES - 1, east_v, 127)):
            held = jnp.zeros((8, 128), f32)
            for cat in range(CATS):
                shift = (cat + 128 - edge) % 128
                column = ice_v[tile, cat, pl.ds(8 + 8 * g, 8), :]
                held = jnp.where(lane == cat, pltpu.roll(column, shift, 1) if shift else column, held)
            target[pl.ds(8 * g, 8), :] = held

    low = pl.ds(0, 8)
    high = pl.ds(ROWS - 8, 8)
    nw_c, ne_c, sw_c, se_c = (corner_v.at[i] for i in range(4))
    to_east = remote(east_v, got_west, 0, 0, (east_b, l))
    to_west = remote(west_v, got_east, 1, 1, (west_b, l))
    to_ne = remote(east_v.at[high], sw_c, 2, 2, (east_b, up))
    to_nw = remote(west_v.at[high], se_c, 3, 3, (west_b, up))
    to_se = remote(east_v.at[low], nw_c, 4, 4, (east_b, down))
    to_sw = remote(west_v.at[low], ne_c, 5, 5, (west_b, down))
    fold_nw = lax.rem(2 * NBLK - b, NBLK)
    fold_ne = lax.rem(2 * NBLK - 2 - b, NBLK)
    nw_home = jnp.logical_and(at_north, fold_nw == b)
    ne_home = jnp.logical_and(at_north, fold_ne == b)
    nw_away = jnp.logical_and(at_north, fold_nw != b)
    ne_away = jnp.logical_and(at_north, fold_ne != b)
    over_nw = remote(west_v.at[high], nw_c, 8, 4, (fold_nw, l))
    over_ne = remote(east_v.at[high], ne_c, 9, 5, (fold_ne, l))
    to_east.start()
    to_west.start()

    @pl.when(inner_north)
    def _():
        to_ne.start()
        to_nw.start()

    @pl.when(inner_south)
    def _():
        to_se.start()
        to_sw.start()

    @pl.when(nw_away)
    def _():
        over_nw.start()

    @pl.when(ne_away)
    def _():
        over_ne.start()

    @pl.when(nw_home)
    def _():
        corner_v[0] = west_v[high, :]

    @pl.when(ne_home)
    def _():
        corner_v[1] = east_v[high, :]

    @pl.when(at_south)
    def _():
        corner_v[2] = jnp.zeros((8, 128), f32)
        corner_v[3] = jnp.zeros((8, 128), f32)

    shares_copy.wait()
    for g in range(GROUPS):
        for t in range(9):
            weight = shares_v[t, pl.ds(8 * g, 8), :].astype(f32) * (1.0 / 4096.0)
            if t % 3 == 2:
                weight = pltpu.roll(weight, 1, 1)
            elif t % 3 == 0:
                weight = pltpu.roll(weight, COLS - 1, 1)
            weights_v[g, t] = weight

    at_first = lane == 0
    at_last = lane == 127
    batch = 6

    def stencil_group(g):
        def stencil(block, carry):
            before = [None] * batch
            held = [None] * batch
            held_right = [None] * batch
            for j in range(TILES + 1):
                if j < TILES:
                    w = [weights_v[g, t, :, pl.ds(128 * j, 128)] for t in range(9)]
                for i in range(batch):
                    cat = block * batch + i
                    if j < TILES:
                        lower = ice_v[j, cat, pl.ds(7 + 8 * g, 8), :]
                        here = ice_v[j, cat, pl.ds(8 + 8 * g, 8), :]
                        upper = ice_v[j, cat, pl.ds(9 + 8 * g, 8), :]
                        centre = w[1] * lower + w[4] * here + w[7] * upper
                        left = w[0] * lower + w[3] * here + w[6] * upper
                        right = w[2] * lower + w[5] * here + w[8] * upper
                        left = pltpu.roll(left, 1, 1)
                        right = pltpu.roll(right, 127, 1)
                    else:
                        right = 0.0
                    if j > 0:
                        moved_ref[cat, pl.ds(8 * g, 8), pl.ds(128 * (j - 1), 128)] = held[i] + jnp.where(
                            at_last, right, held_right[i]
                        )
                    if j < TILES:
                        held[i] = centre + jnp.where(at_first, 0.0 if j == 0 else before[i], left)
                        before[i] = left
                        held_right[i] = right
            return carry

        lax.fori_loop(0, CATS // batch, stencil, 0)

    stencil_group(0)

    for k in range(1, NLAT):
        lat_copy(k).wait_recv()
    for part in range(NBLK):
        for half in range(2):
            for q in range(2):
                turn_v[pl.ds(32 * part + 16 * q + half, 8, stride=2), :] = mid_v[
                    pl.ds(2 * part + half + 128 * q, 8, stride=16), :
                ]

    def blk_copy(k):
        peer = lax.rem(b + k, NBLK)
        return pltpu.make_async_remote_copy(
            src_ref=turn_v.at[pl.ds(pl.multiple_of(32 * peer, 32), 32), :],
            dst_ref=rate_ref.at[pl.ds(pl.multiple_of(32 * b, 32), 32), :],
            send_sem=blk_send.at[k], recv_sem=blk_recv.at[k],
            device_id=(peer, l), device_id_type=MESH,
        )

    for k in range(1, NBLK):
        blk_copy(k).start()
    own = pl.ds(pl.multiple_of(32 * b, 32), 32)
    rate_ref[own, :] = turn_v[own, :]

    for g in (1, 2, 3):
        stencil_group(g)

    to_east.wait()
    to_west.wait()

    @pl.when(inner_north)
    def _():
        to_ne.wait_send()
        to_nw.wait_send()
        to_se.wait_recv()
        to_sw.wait_recv()

    @pl.when(inner_south)
    def _():
        to_se.wait_send()
        to_sw.wait_send()
        to_ne.wait_recv()
        to_nw.wait_recv()

    @pl.when(nw_away)
    def _():
        over_nw.wait()

    @pl.when(ne_away)
    def _():
        over_ne.wait()

    top_west = jnp.where(at_north, corner_v[0, pl.ds(7, 1), :], corner_v[0, pl.ds(0, 1), :])
    top_east = jnp.where(at_north, corner_v[1, pl.ds(7, 1), :], corner_v[1, pl.ds(0, 1), :])
    for source, target, lower, upper, t, spot in (
        (got_west, west_h, corner_v[2, pl.ds(7, 1), :], top_west, 0, 0),
        (got_east, east_h, corner_v[3, pl.ds(7, 1), :], top_east, 2, 127),
    ):
        target[pl.ds(8, ROWS), :] = source[...]
        target[pl.ds(7, 1), :] = lower
        target[pl.ds(8 + ROWS, 1), :] = upper
        tile = pl.ds(0 if spot == 0 else COLS - 128, 128)
        for g in range(GROUPS):
            rows = pl.ds(8 * g, 8)
            total = jnp.zeros((8, 128), f32)
            for dy in range(3):
                weight = shares_v[3 * dy + t, rows, tile].astype(f32) * (1.0 / 4096.0)
                total = total + weight[:, spot : spot + 1] * target[pl.ds(7 + dy + 8 * g, 8), :]
            source[rows, :] = total

    def columns(block, carry):
        for i in range(6):
            cat = block * 6 + i
            for g in range(GROUPS):
                rows = pl.ds(8 * g, 8)
                west = pltpu.roll(got_west[rows, :], jnp.bitwise_and(128 - cat, 127), 1)
                east = pltpu.roll(got_east[rows, :], 127 - cat, 1)
                moved_ref[cat, rows, pl.ds(0, 128)] += jnp.where(at_first, west, 0.0)
                moved_ref[cat, rows, pl.ds(COLS - 128, 128)] += jnp.where(at_last, east, 0.0)
        return carry

    lax.fori_loop(0, CATS // 6, columns, 0)

    @pl.when(inner_south)
    def _():
        to_south.wait_send()
        to_north.wait_recv()

    @pl.when(at_south)
    def _():
        got_south[...] = jnp.zeros_like(got_south)

    @pl.when(inner_north)
    def _():
        to_north.wait_send()
        to_south.wait_recv()

    @pl.when(at_north)
    def _():
        over.wait()
        first = lax.broadcasted_iota(jnp.int32, (128, 128), 0)
        second = lax.broadcasted_iota(jnp.int32, (128, 128), 1)
        mirror = (first + second == 127).astype(f32)
        for j in range(TILES // 2):
            one = pl.ds(128 * j, 128)
            other = pl.ds(128 * (TILES - 1 - j), 128)
            turned = [
                jnp.dot(got_north[:, lanes], mirror, precision=lax.Precision.HIGHEST, preferred_element_type=f32)
                for lanes in (other, one)
            ]
            got_north[:, one] = turned[0]
            got_north[:, other] = turned[1]

    place_x = lax.broadcasted_iota(jnp.int32, (1, COLS), 1)
    for source, t, spot in ((got_south, 0, 0), (got_north, 6, ROWS - 1)):
        weight = [shares_v[t + dx, pl.ds(spot, 1), :].astype(f32) * (1.0 / 4096.0) for dx in range(3)]
        weight[0] = jnp.where(place_x == 0, 0.0, weight[0])
        weight[2] = jnp.where(place_x == COLS - 1, 0.0, weight[2])
        for first in range(0, CATS, 8):
            size = min(8, CATS - first)
            line = source[pl.ds(first, size), :]
            added = weight[1] * line + weight[0] * pltpu.roll(line, 1, 1) + weight[2] * pltpu.roll(line, COLS - 1, 1)
            for j in range(TILES):
                lanes = pl.ds(128 * j, 128)
                moved_ref[pl.ds(first, size), spot, lanes] += added[:, 128 * j : 128 * (j + 1)]

    for k in range(1, NLAT):
        lat_copy(k).wait_send()
    for k in range(1, NBLK):
        blk_copy(k).wait()


def front(route, wave, ice, shares):
    f32 = jnp.float32
    dma = pltpu.SemaphoreType.DMA
    return pl.pallas_call(
        front_kernel,
        name="front",
        out_shape=(pltpu.VMEM((CATS, ROWS, COLS), f32), pltpu.VMEM((FLAT, 128), f32)),
        in_specs=[any_spec()] * 4,
        out_specs=(vmem_spec(), vmem_spec()),
        scratch_shapes=[
            pltpu.VMEM((FREQ, PEERS, 256), f32),
            pltpu.VMEM((2, PEERS, 128), f32),
            pltpu.VMEM((FLAT, 128), f32),
            pltpu.VMEM((FLAT, 128), f32),
            pltpu.VMEM((FLAT, 128), f32),
            pltpu.VMEM((TILES, CATS, ROWS + 16, 128), f32),
            pltpu.VMEM((9, ROWS, COLS), jnp.int32),
            pltpu.VMEM((GROUPS, 9, 8, COLS), f32),
            pltpu.VMEM((CATS, COLS), f32),
            pltpu.VMEM((CATS, COLS), f32),
            pltpu.VMEM((CATS, COLS), f32),
            pltpu.VMEM((CATS, COLS), f32),
            pltpu.VMEM((ROWS, 128), f32),
            pltpu.VMEM((ROWS, 128), f32),
            pltpu.VMEM((ROWS, 128), f32),
            pltpu.VMEM((ROWS, 128), f32),
            pltpu.VMEM((4, 8, 128), f32),
            pltpu.VMEM((ROWS + 16, 128), f32),
            pltpu.VMEM((ROWS + 16, 128), f32),
            pltpu.VMEM((1, PEERS), jnp.int32),
            dma,
            dma((4,)),
            dma((GROUPS, TILES)),
            dma,
            dma((NLAT,)),
            dma((NLAT,)),
            dma((NBLK,)),
            dma((NBLK,)),
            dma((11,)),
            dma((8,)),
        ],
        compiler_params=pltpu.CompilerParams(
            collective_id=0, has_side_effects=True, vmem_limit_bytes=FRONT_LIMIT
        ),
    )(*(pltpu.with_memory_space_constraint(x, pltpu.HBM) for x in (route, wave, ice, shares)))


def physics(area, weld, crack):
    grown = [None] * NFSD
    lost = None
    for k in range(NFSD):
        total = None
        for d in range(1, NFSD):
            below, above = k - d, k + d
            if below >= 0 and above < NFSD:
                term = (area[below] - area[above]) * (1.0 / (1.0 + d))
            elif below >= 0:
                term = area[below] * (1.0 / (1.0 + d))
            elif above < NFSD:
                term = area[above] * (-1.0 / (1.0 + d))
            else:
                continue
            total = term if total is None else total + term
        rate = weld * area[k]
        value = area[k] + rate * total
        if k > 0:
            value = value + lost
        if k < NFSD - 1:
            lost = rate * area[k]
            value = value - lost
        grown[k] = value
    result = [None] * NFSD
    above = None
    for k in range(NFSD - 1, -1, -1):
        scaled = crack * grown[k]
        value = grown[k] - scaled * float(k) if k > 0 else grown[k]
        if above is not None:
            value = value + above
        above = scaled if above is None else above + scaled
        result[k] = value
    return result


def back_kernel(moved_ref, weld_ref, cover_ref, rate_ref, out_hbm, out_v, weld_v, crack_v, out_sem):
    for g in range(GROUPS):
        rows = pl.ds(8 * g, 8)
        mine = lax.broadcasted_iota(jnp.int32, (8, ROWS), 0) + 8 * g == lax.broadcasted_iota(jnp.int32, (8, ROWS), 1)
        listed = jnp.broadcast_to((cover_ref[...] > 0).astype(jnp.float32), (8, ROWS))
        covered = jnp.sum(jnp.where(mine, listed, 0.0), axis=1, keepdims=True)
        weld_v[rows, :] = weld_ref[rows, :] * covered * 0.06
        for j in range(TILES):
            crack_v[rows, pl.ds(128 * j, 128)] = (
                rate_ref[pl.ds(64 * g + j, 8, stride=8), :] * covered * (0.1 / 11.0 / FREQ)
            )

    def out_copy(g):
        rows = pl.ds(8 * g, 8)
        return pltpu.make_async_copy(out_v.at[:, rows, :], out_hbm.at[:, rows, :], out_sem.at[g])

    for g in range(GROUPS):
        rows = pl.ds(8 * g, 8)

        def column(j, carry):
            lanes = pl.ds(pl.multiple_of(128 * j, 128), 128)
            weld = weld_v[rows, lanes]
            crack = crack_v[rows, lanes]
            for n in range(NCAT):
                area = [moved_ref[NFSD * n + k, rows, lanes] for k in range(NFSD)]
                result = physics(area, weld, crack * (1.0 / (1.0 + 0.5 * n)))
                for k in range(NFSD):
                    out_v[NFSD * n + k, rows, lanes] = result[k]
            return carry

        lax.fori_loop(0, TILES, column, 0)
        out_copy(g).start()

    for g in range(GROUPS):
        out_copy(g).wait()


def back(moved, weld, cover, rate):
    f32 = jnp.float32
    return pl.pallas_call(
        back_kernel,
        name="back",
        out_shape=jax.ShapeDtypeStruct((CATS, ROWS, COLS), f32),
        in_specs=[vmem_spec()] * 4,
        out_specs=any_spec(),
        scratch_shapes=[
            pltpu.VMEM((CATS, ROWS, COLS), f32),
            pltpu.VMEM((ROWS, COLS), f32),
            pltpu.VMEM((ROWS, COLS), f32),
            pltpu.SemaphoreType.DMA((GROUPS,)),
        ],
        compiler_params=pltpu.CompilerParams(vmem_limit_bytes=BACK_LIMIT),
    )(moved, weld, cover, rate)


def on_device(ice_area, departure_weights, weld_rate, ice_cover, wave_ocean, ocean_route):
    ice = ice_area.reshape(CATS, ROWS, COLS)
    moved, rate = front(ocean_route, wave_ocean[0], ice, departure_weights)
    out = back(moved, weld_rate, ice_cover.reshape(1, ROWS), rate)
    return out.reshape(ice_area.shape)


def solution(mesh):
    return jax.shard_map(
        on_device,
        mesh=mesh,
        in_specs=(
            P(None, None, "lat", "blk"),
            P(None, "lat", "blk"),
            P("lat", "blk"),
            P("lat", "blk"),
            P(("blk", "lat"), None, None, None),
            P(("blk", "lat"), None),
        ),
        out_specs=P(None, None, "lat", "blk"),
        check_vma=False,
    )
```

profile of v0, /device:TPU:24, one launch (start us, length us, event | category | flops | bytes accessed | tf_op | source)
XLA Modules:
  0.0 32.0 jit_solution(14084674617645784378)
XLA Ops:
  0.0 0.0 copy-start.1
  0.0 0.0 copy-start
  0.0 23.0 %front.1 = (f32[60,32,1024]{2,1,0:T(8,128)S(1)}, f32[256,128]{1,0:T(8,128)S(1)}) custom-call(s32[1,128]{1,0:T(1,128)} %route_hbm.1, f32[25,128,256]{2,1,0:T(8,128)} %bitcast.6, f32[60,32,1024]{2,1,0:T(8,128)} %bitcast.5, s32[9,32,1024]{2,1,0:T(8,128)} %shares_hbm.1), custom_call_target="tpu_custom_call" | custom-call | tf_op jit(solution)/shard_map/front/pallas_call | solution.py:416
  23.0 0.0 copy-done.1
  23.0 0.0 copy-done
  23.0 9.0 %back.1 = f32[60,32,1024]{2,1,0:T(8,128)} custom-call(f32[60,32,1024]{2,1,0:T(8,128)S(1)} %get-tuple-element.7.moved_ref, f32[32,1024]{1,0:T(8,128)S(1)} %copy-done, s32[1,32]{1,0:T(1,128)S(1)} %bitcast.4, f32[256,128]{1,0:T(8,128)S(1)} %get-tuple-element.8.rate_ref), custom_call_target="tpu_custom_call" | custom-call | tf_op jit(solution)/shard_map/back/pallas_call | solution.py:535
Async XLA Ops:
  0.0 23.0 %copy-start.1 = (s32[32,1]{0,1:T(1,128)S(1)}, s32[32,1]{0,1:T(1,128)}, u32[]{:S(2)}) copy-start(s32[32,1]{0,1:T(1,128)} %param.9) | copy-start | bytes 388
  0.0 23.0 %copy-start = (f32[32,1024]{1,0:T(8,128)S(1)}, f32[32,1024]{1,0:T(8,128)}, u32[]{:S(2)}) copy-start(f32[32,1024]{1,0:T(8,128)} %weld_ref.1) | copy-start | bytes 393220
where the time goes:
time: 32.1 us; the launch traced here: 32 us
  Pallas kernels  32 us (100%)
    pallas_call x1, Pallas kernels, front(): pl.pallas_call(front_kernel, name='front', out_shape=(pltpu.VMEM((CATS, R...  23 us
    pallas_call x1, Pallas kernels, back(): pl.pallas_call(back_kernel, name='back', out_shape=jax.ShapeDtypeStruct((...  8.96 us

commit v1 on v0

--- a/solution.py
+++ b/solution.py
@@ -30,10 +30,43 @@
     return pl.BlockSpec(memory_space=pltpu.HBM)
 
 
-def front_kernel(route_hbm, wave_hbm, ice_hbm, shares_hbm, moved_ref, rate_ref,
+def covered_rows(cover, g):
+    listed = jnp.broadcast_to((cover > 0).astype(jnp.float32), (8, ROWS))
+    mine = lax.broadcasted_iota(jnp.int32, (8, ROWS), 0) + 8 * g == lax.broadcasted_iota(jnp.int32, (8, ROWS), 1)
+    return jnp.sum(jnp.where(mine, listed, 0.0), axis=1, keepdims=True)
+
+
+def welded(area, weld):
+    grown = [None] * NFSD
+    lost = None
+    for k in range(NFSD):
+        total = None
+        for d in range(1, NFSD):
+            below, above = k - d, k + d
+            if below >= 0 and above < NFSD:
+                term = (area[below] - area[above]) * (1.0 / (1.0 + d))
+            elif below >= 0:
+                term = area[below] * (1.0 / (1.0 + d))
+            elif above < NFSD:
+                term = area[above] * (-1.0 / (1.0 + d))
+            else:
+                continue
+            total = term if total is None else total + term
+        rate = weld * area[k]
+        value = area[k] + rate * total
+        if k > 0:
+            value = value + lost
+        if k < NFSD - 1:
+            lost = rate * area[k]
+            value = value - lost
+        grown[k] = value
+    return grown
+
+
+def front_kernel(route_hbm, wave_hbm, ice_hbm, shares_hbm, weld_hbm, cover_hbm, moved_ref, rate_ref,
                  wave_v, sums_v, send_v, mid_v, turn_v, ice_v, shares_v, weights_v,
                  south_v, north_v, got_south, got_north, west_v, east_v, got_west, got_east, corner_v,
-                 west_h, east_h, route_v, route_sem, wave_sem, ice_sem, shares_sem,
+                 west_h, east_h, weld_v, cover_v, route_v, weld_sem, route_sem, wave_sem, ice_sem, shares_sem,
                  lat_send, lat_recv, blk_send, blk_recv, send_sem, recv_sem):
     f32 = jnp.float32
     b = lax.axis_index("blk")
@@ -46,6 +79,8 @@
     inner_south = l > 0
     up = jnp.minimum(l + 1, NLAT - 1)
     down = jnp.maximum(l - 1, 0)
+    ahead = jnp.logical_or(b < NBLK // 2, l // 4 + lax.rem(l, 4) <= 3)
+    behind = jnp.logical_not(ahead)
 
     parts = 4
     share = PEERS // parts
@@ -55,24 +90,27 @@
         )
         for i in range(parts)
     ]
-    ice_copies = {
-        (g, j): pltpu.make_async_copy(
-            ice_hbm.at[:, pl.ds(8 * g, 8), pl.ds(128 * j, 128)],
-            ice_v.at[j, :, pl.ds(8 + 8 * g, 8), :],
-            ice_sem.at[g, j],
+    def ice_copy(part, j):
+        first, size = ((0, 8), (8, ROWS - 16), (ROWS - 8, 8))[part]
+        return pltpu.make_async_copy(
+            ice_hbm.at[:, pl.ds(first, size), pl.ds(128 * j, 128)],
+            ice_v.at[j, :, pl.ds(8 + first, size), :],
+            ice_sem.at[part, j],
         )
-        for g in range(GROUPS)
-        for j in range(TILES)
-    }
+
     shares_copy = pltpu.make_async_copy(shares_hbm, shares_v, shares_sem)
     route_copy = pltpu.make_async_copy(route_hbm, route_v, route_sem)
-    for copy in [route_copy] + wave_copies:
+    weld_copy = pltpu.make_async_copy(weld_hbm, weld_v, weld_sem.at[0])
+    cover_copy = pltpu.make_async_copy(cover_hbm, cover_v, weld_sem.at[1])
+    for part in (0, 2):
+        for j in range(TILES):
+            ice_copy(part, j).start()
+    for copy in [route_copy] + wave_copies + [shares_copy]:
         copy.start()
-    for g in (0, 3, 1, 2):
-        for j in range(TILES):
-            ice_copies[g, j].start()
-        if g == 3:
-            shares_copy.start()
+    for j in range(TILES):
+        ice_copy(1, j).start()
+    weld_copy.start()
+    cover_copy.start()
 
     barrier = pltpu.get_barrier_semaphore()
 
@@ -87,11 +125,40 @@
         greet((side, lax.rem(l + 1, NLAT)))
         greet((side, lax.rem(l + NLAT - 1, NLAT)))
 
-    for j in range(TILES):
+    def remote(source, target, sent, got, dev):
+        return pltpu.make_async_remote_copy(
+            src_ref=source, dst_ref=target, send_sem=send_sem.at[sent], recv_sem=recv_sem.at[got],
+            device_id=dev, device_id_type=MESH,
+        )
+
+    for part, spot, target in ((0, 8, south_v), (2, 7 + ROWS, north_v)):
+        for j in range(TILES):
+            ice_copy(part, j).wait()
         for first in range(0, CATS, 8):
             size = min(8, CATS - first)
-            for spot in (7, 8 + ROWS):
-                ice_v[j, pl.ds(first, size), spot, :] = jnp.zeros((size, 128), f32)
+            for j in range(TILES):
+                target[pl.ds(first, size), pl.ds(128 * j, 128)] = ice_v[j, pl.ds(first, size), spot, :]
+
+    to_south = remote(south_v, got_north, 6, 6, (b, down))
+    to_north = remote(north_v, got_south, 7, 7, (b, up))
+    over = remote(north_v, got_north, 10, 6, (NBLK - 1 - b, l))
+
+    def send_rows():
+        pl.semaphore_wait(barrier, NLAT - 1 + NBLK - 1 + 4)
+
+        @pl.when(inner_south)
+        def _():
+            to_south.start()
+
+        @pl.when(inner_north)
+        def _():
+            to_north.start()
+
+        @pl.when(at_north)
+        def _():
+            over.start()
+
+    pl.when(behind)(send_rows)
 
     for i in range(parts):
         wave_copies[i].wait()
@@ -110,7 +177,7 @@
 
     route_copy.wait()
     route = route_v[...]
-    place = (jnp.bitwise_and(route, NLAT - 1) * NBLK + jnp.right_shift(route, 4)) * 2
+    place = 2 * route
     row = lax.broadcasted_iota(jnp.int32, (FLAT, PEERS), 0)
     ordered = jnp.zeros((FLAT, 128), f32)
     for half in range(2):
@@ -120,57 +187,34 @@
         )
     send_v[...] = ordered
 
-    pl.semaphore_wait(barrier, NLAT - 1 + NBLK - 1 + 4)
-
-    def lat_copy(k):
-        peer = lax.rem(l + k, NLAT)
+    def blk_copy(k):
+        peer = lax.rem(b + k, NBLK)
         return pltpu.make_async_remote_copy(
-            src_ref=send_v.at[pl.ds(pl.multiple_of(16 * peer, 16), 16), :],
-            dst_ref=mid_v.at[pl.ds(pl.multiple_of(16 * l, 16), 16), :],
-            send_sem=lat_send.at[k], recv_sem=lat_recv.at[k],
-            device_id=(b, peer), device_id_type=MESH,
+            src_ref=send_v.at[pl.ds(pl.multiple_of(32 * peer, 32), 32), :],
+            dst_ref=mid_v.at[pl.ds(pl.multiple_of(32 * b, 32), 32), :],
+            send_sem=blk_send.at[k], recv_sem=blk_recv.at[k],
+            device_id=(peer, l), device_id_type=MESH,
         )
 
-    for k in range(1, NLAT):
-        lat_copy(k).start()
-    mine = pl.ds(pl.multiple_of(16 * l, 16), 16)
-    mid_v[mine, :] = send_v[mine, :]
-
-    def remote(source, target, sent, got, dev):
-        return pltpu.make_async_remote_copy(
-            src_ref=source, dst_ref=target, send_sem=send_sem.at[sent], recv_sem=recv_sem.at[got],
-            device_id=dev, device_id_type=MESH,
-        )
-
-    for g, spot, target in ((0, 8, south_v), (3, 7 + ROWS, north_v)):
-        for j in range(TILES):
-            ice_copies[g, j].wait()
+    def send_waves():
+        for k in range(1, NBLK):
+            blk_copy(k).start()
+
+    pl.when(behind)(send_waves)
+    own = pl.ds(pl.multiple_of(32 * b, 32), 32)
+    mid_v[own, :] = send_v[own, :]
+
+    for j in range(TILES):
         for first in range(0, CATS, 8):
             size = min(8, CATS - first)
-            for j in range(TILES):
-                target[pl.ds(first, size), pl.ds(128 * j, 128)] = ice_v[j, pl.ds(first, size), spot, :]
-
-    to_south = remote(south_v, got_north, 6, 6, (b, down))
-    to_north = remote(north_v, got_south, 7, 7, (b, up))
-    over = remote(north_v, got_north, 10, 6, (NBLK - 1 - b, l))
-
-    @pl.when(inner_south)
-    def _():
-        to_south.start()
-
-    @pl.when(inner_north)
-    def _():
-        to_north.start()
-
-    @pl.when(at_north)
-    def _():
-        over.start()
+            for spot in (7, 8 + ROWS):
+                ice_v[j, pl.ds(first, size), spot, :] = jnp.zeros((size, 128), f32)
 
     lane = lax.broadcasted_iota(jnp.int32, (8, 128), 1)
     for g in (0, 3, 1, 2):
-        if g in (1, 2):
+        if g == 1:
             for j in range(TILES):
-                ice_copies[g, j].wait()
+                ice_copy(1, j).wait()
         for tile, target, edge in ((0, west_v, 0), (TILES - 1, east_v, 127)):
             held = jnp.zeros((8, 128), f32)
             for cat in range(CATS):
@@ -196,26 +240,29 @@
     ne_away = jnp.logical_and(at_north, fold_ne != b)
     over_nw = remote(west_v.at[high], nw_c, 8, 4, (fold_nw, l))
     over_ne = remote(east_v.at[high], ne_c, 9, 5, (fold_ne, l))
-    to_east.start()
-    to_west.start()
-
-    @pl.when(inner_north)
-    def _():
-        to_ne.start()
-        to_nw.start()
-
-    @pl.when(inner_south)
-    def _():
-        to_se.start()
-        to_sw.start()
-
-    @pl.when(nw_away)
-    def _():
-        over_nw.start()
-
-    @pl.when(ne_away)
-    def _():
-        over_ne.start()
+    def send_columns():
+        to_east.start()
+        to_west.start()
+
+        @pl.when(inner_north)
+        def _():
+            to_ne.start()
+            to_nw.start()
+
+        @pl.when(inner_south)
+        def _():
+            to_se.start()
+            to_sw.start()
+
+        @pl.when(nw_away)
+        def _():
+            over_nw.start()
+
+        @pl.when(ne_away)
+        def _():
+            over_ne.start()
+
+    pl.when(behind)(send_columns)
 
     @pl.when(nw_home)
     def _():
@@ -239,6 +286,12 @@
             elif t % 3 == 0:
                 weight = pltpu.roll(weight, COLS - 1, 1)
             weights_v[g, t] = weight
+
+    @pl.when(ahead)
+    def _():
+        send_rows()
+        send_columns()
+        send_waves()
 
     at_first = lane == 0
     at_last = lane == 127
@@ -279,31 +332,28 @@
 
     stencil_group(0)
 
-    for k in range(1, NLAT):
-        lat_copy(k).wait_recv()
-    for part in range(NBLK):
-        for half in range(2):
-            for q in range(2):
-                turn_v[pl.ds(32 * part + 16 * q + half, 8, stride=2), :] = mid_v[
-                    pl.ds(2 * part + half + 128 * q, 8, stride=16), :
-                ]
-
-    def blk_copy(k):
-        peer = lax.rem(b + k, NBLK)
-        return pltpu.make_async_remote_copy(
-            src_ref=turn_v.at[pl.ds(pl.multiple_of(32 * peer, 32), 32), :],
-            dst_ref=rate_ref.at[pl.ds(pl.multiple_of(32 * b, 32), 32), :],
-            send_sem=blk_send.at[k], recv_sem=blk_recv.at[k],
-            device_id=(peer, l), device_id_type=MESH,
-        )
-
-    for k in range(1, NBLK):
-        blk_copy(k).start()
-    own = pl.ds(pl.multiple_of(32 * b, 32), 32)
-    rate_ref[own, :] = turn_v[own, :]
-
     for g in (1, 2, 3):
         stencil_group(g)
+
+    for k in range(1, NBLK):
+        blk_copy(k).wait_recv()
+    for part in range(NLAT):
+        for half in range(2):
+            turn_v[pl.ds(16 * part + half, 8, stride=2), :] = mid_v[pl.ds(2 * part + half, 8, stride=32), :]
+
+    def lat_copy(k):
+        peer = lax.rem(l + k, NLAT)
+        return pltpu.make_async_remote_copy(
+            src_ref=turn_v.at[pl.ds(pl.multiple_of(16 * peer, 16), 16), :],
+            dst_ref=rate_ref.at[pl.ds(pl.multiple_of(16 * l, 16), 16), :],
+            send_sem=lat_send.at[k], recv_sem=lat_recv.at[k],
+            device_id=(b, peer), device_id_type=MESH,
+        )
+
+    for k in range(1, NLAT):
+        lat_copy(k).start()
+    mine = pl.ds(pl.multiple_of(16 * l, 16), 16)
+    rate_ref[mine, :] = turn_v[mine, :]
 
     to_east.wait()
     to_west.wait()
@@ -348,18 +398,35 @@
                 total = total + weight[:, spot : spot + 1] * target[pl.ds(7 + dy + 8 * g, 8), :]
             source[rows, :] = total
 
-    def columns(block, carry):
-        for i in range(6):
-            cat = block * 6 + i
-            for g in range(GROUPS):
-                rows = pl.ds(8 * g, 8)
-                west = pltpu.roll(got_west[rows, :], jnp.bitwise_and(128 - cat, 127), 1)
-                east = pltpu.roll(got_east[rows, :], 127 - cat, 1)
-                moved_ref[cat, rows, pl.ds(0, 128)] += jnp.where(at_first, west, 0.0)
-                moved_ref[cat, rows, pl.ds(COLS - 128, 128)] += jnp.where(at_last, east, 0.0)
+    for g in range(GROUPS):
+        rows = pl.ds(8 * g, 8)
+        west = got_west[rows, :]
+        east = got_east[rows, :]
+        for cat in range(CATS):
+            first = pltpu.roll(west, 128 - cat, 1) if cat else west
+            moved_ref[cat, rows, pl.ds(0, 128)] += jnp.where(at_first, first, 0.0)
+            last = pltpu.roll(east, 127 - cat, 1)
+            moved_ref[cat, rows, pl.ds(COLS - 128, 128)] += jnp.where(at_last, last, 0.0)
+
+    weld_copy.wait()
+    cover_copy.wait()
+    for g in range(GROUPS):
+        rows = pl.ds(8 * g, 8)
+        weld_v[rows, :] = weld_v[rows, :] * (covered_rows(cover_v[...], g) * 0.06)
+
+    def weld_part(part, carry):
+        group = part // NCAT
+        n = part - NCAT * group
+        rows = pl.ds(pl.multiple_of(8 * group, 8), 8)
+        for j in range(TILES):
+            lanes = pl.ds(128 * j, 128)
+            area = [moved_ref[NFSD * n + k, rows, lanes] for k in range(NFSD)]
+            grown = welded(area, weld_v[rows, lanes])
+            for k in range(NFSD):
+                moved_ref[NFSD * n + k, rows, lanes] = grown[k]
         return carry
 
-    lax.fori_loop(0, CATS // 6, columns, 0)
+    lax.fori_loop(NCAT, 3 * NCAT, weld_part, 0)
 
     @pl.when(inner_south)
     def _():
@@ -404,20 +471,23 @@
                 lanes = pl.ds(128 * j, 128)
                 moved_ref[pl.ds(first, size), spot, lanes] += added[:, 128 * j : 128 * (j + 1)]
 
+    lax.fori_loop(0, NCAT, weld_part, 0)
+    lax.fori_loop(3 * NCAT, 4 * NCAT, weld_part, 0)
+
+    for k in range(1, NBLK):
+        blk_copy(k).wait_send()
     for k in range(1, NLAT):
-        lat_copy(k).wait_send()
-    for k in range(1, NBLK):
-        blk_copy(k).wait()
-
-
-def front(route, wave, ice, shares):
+        lat_copy(k).wait()
+
+
+def front(route, wave, ice, shares, weld, cover):
     f32 = jnp.float32
     dma = pltpu.SemaphoreType.DMA
     return pl.pallas_call(
         front_kernel,
         name="front",
         out_shape=(pltpu.VMEM((CATS, ROWS, COLS), f32), pltpu.VMEM((FLAT, 128), f32)),
-        in_specs=[any_spec()] * 4,
+        in_specs=[any_spec()] * 6,
         out_specs=(vmem_spec(), vmem_spec()),
         scratch_shapes=[
             pltpu.VMEM((FREQ, PEERS, 256), f32),
@@ -439,10 +509,13 @@
             pltpu.VMEM((4, 8, 128), f32),
             pltpu.VMEM((ROWS + 16, 128), f32),
             pltpu.VMEM((ROWS + 16, 128), f32),
+            pltpu.VMEM((ROWS, COLS), f32),
+            pltpu.VMEM((1, ROWS), jnp.int32),
             pltpu.VMEM((1, PEERS), jnp.int32),
+            dma((2,)),
             dma,
             dma((4,)),
-            dma((GROUPS, TILES)),
+            dma((3, TILES)),
             dma,
             dma((NLAT,)),
             dma((NLAT,)),
@@ -454,33 +527,10 @@
         compiler_params=pltpu.CompilerParams(
             collective_id=0, has_side_effects=True, vmem_limit_bytes=FRONT_LIMIT
         ),
-    )(*(pltpu.with_memory_space_constraint(x, pltpu.HBM) for x in (route, wave, ice, shares)))
-
-
-def physics(area, weld, crack):
-    grown = [None] * NFSD
-    lost = None
-    for k in range(NFSD):
-        total = None
-        for d in range(1, NFSD):
-            below, above = k - d, k + d
-            if below >= 0 and above < NFSD:
-                term = (area[below] - area[above]) * (1.0 / (1.0 + d))
-            elif below >= 0:
-                term = area[below] * (1.0 / (1.0 + d))
-            elif above < NFSD:
-                term = area[above] * (-1.0 / (1.0 + d))
-            else:
-                continue
-            total = term if total is None else total + term
-        rate = weld * area[k]
-        value = area[k] + rate * total
-        if k > 0:
-            value = value + lost
-        if k < NFSD - 1:
-            lost = rate * area[k]
-            value = value - lost
-        grown[k] = value
+    )(*(pltpu.with_memory_space_constraint(x, pltpu.HBM) for x in (route, wave, ice, shares, weld, cover)))
+
+
+def cracked(grown, crack):
     result = [None] * NFSD
     above = None
     for k in range(NFSD - 1, -1, -1):
@@ -493,65 +543,65 @@
     return result
 
 
-def back_kernel(moved_ref, weld_ref, cover_ref, rate_ref, out_hbm, out_v, weld_v, crack_v, out_sem):
+def back_kernel(welded_ref, cover_ref, rate_ref, out_hbm, out_v, crack_v, out_sem):
     for g in range(GROUPS):
         rows = pl.ds(8 * g, 8)
-        mine = lax.broadcasted_iota(jnp.int32, (8, ROWS), 0) + 8 * g == lax.broadcasted_iota(jnp.int32, (8, ROWS), 1)
-        listed = jnp.broadcast_to((cover_ref[...] > 0).astype(jnp.float32), (8, ROWS))
-        covered = jnp.sum(jnp.where(mine, listed, 0.0), axis=1, keepdims=True)
-        weld_v[rows, :] = weld_ref[rows, :] * covered * 0.06
+        covered = covered_rows(cover_ref[...], g)
         for j in range(TILES):
-            crack_v[rows, pl.ds(128 * j, 128)] = (
-                rate_ref[pl.ds(64 * g + j, 8, stride=8), :] * covered * (0.1 / 11.0 / FREQ)
-            )
-
-    def out_copy(g):
-        rows = pl.ds(8 * g, 8)
-        return pltpu.make_async_copy(out_v.at[:, rows, :], out_hbm.at[:, rows, :], out_sem.at[g])
-
-    for g in range(GROUPS):
-        rows = pl.ds(8 * g, 8)
-
-        def column(j, carry):
-            lanes = pl.ds(pl.multiple_of(128 * j, 128), 128)
-            weld = weld_v[rows, lanes]
-            crack = crack_v[rows, lanes]
-            for n in range(NCAT):
-                area = [moved_ref[NFSD * n + k, rows, lanes] for k in range(NFSD)]
-                result = physics(area, weld, crack * (1.0 / (1.0 + 0.5 * n)))
-                for k in range(NFSD):
-                    out_v[NFSD * n + k, rows, lanes] = result[k]
-            return carry
-
-        lax.fori_loop(0, TILES, column, 0)
-        out_copy(g).start()
-
-    for g in range(GROUPS):
-        out_copy(g).wait()
-
-
-def back(moved, weld, cover, rate):
+            for half in range(2):
+                crack_v[pl.ds(8 * g + 4 * half, 4), pl.ds(128 * j, 128)] = rate_ref[
+                    pl.ds(16 * (j // 2) + 4 * g + 2 * half + j % 2, 4, stride=64), :
+                ]
+        crack_v[rows, :] = crack_v[rows, :] * covered * (0.1 / 11.0 / FREQ)
+
+    def out_copy(part):
+        group = part // NCAT
+        cats = pl.ds(NFSD * (part - NCAT * group), NFSD)
+        rows = pl.ds(pl.multiple_of(8 * group, 8), 8)
+        return pltpu.make_async_copy(out_v.at[cats, rows, :], out_hbm.at[cats, rows, :], out_sem.at[part])
+
+    def chunk(part, carry):
+        group = part // NCAT
+        n = part - NCAT * group
+        rows = pl.ds(pl.multiple_of(8 * group, 8), 8)
+        thick = 1.0 / (1.0 + 0.5 * jnp.full((8, 128), n, jnp.int32).astype(jnp.float32))
+        for j in range(TILES):
+            lanes = pl.ds(128 * j, 128)
+            grown = [welded_ref[NFSD * n + k, rows, lanes] for k in range(NFSD)]
+            result = cracked(grown, crack_v[rows, lanes] * thick)
+            for k in range(NFSD):
+                out_v[NFSD * n + k, rows, lanes] = result[k]
+        out_copy(part).start()
+        return carry
+
+    parts = GROUPS * NCAT
+    lax.fori_loop(0, parts, chunk, 0)
+    for part in range(parts):
+        out_copy(part).wait()
+
+
+def back(grown, cover, rate):
     f32 = jnp.float32
     return pl.pallas_call(
         back_kernel,
         name="back",
         out_shape=jax.ShapeDtypeStruct((CATS, ROWS, COLS), f32),
-        in_specs=[vmem_spec()] * 4,
+        in_specs=[vmem_spec()] * 3,
         out_specs=any_spec(),
         scratch_shapes=[
             pltpu.VMEM((CATS, ROWS, COLS), f32),
             pltpu.VMEM((ROWS, COLS), f32),
-            pltpu.VMEM((ROWS, COLS), f32),
-            pltpu.SemaphoreType.DMA((GROUPS,)),
+            pltpu.SemaphoreType.DMA((GROUPS * NCAT,)),
         ],
         compiler_params=pltpu.CompilerParams(vmem_limit_bytes=BACK_LIMIT),
-    )(moved, weld, cover, rate)
+    )(grown, cover, rate)
 
 
 def on_device(ice_area, departure_weights, weld_rate, ice_cover, wave_ocean, ocean_route):
     ice = ice_area.reshape(CATS, ROWS, COLS)
-    moved, rate = front(ocean_route, wave_ocean[0], ice, departure_weights)
-    out = back(moved, weld_rate, ice_cover.reshape(1, ROWS), rate)
+    cover = ice_cover.reshape(1, ROWS)
+    grown, rate = front(ocean_route, wave_ocean[0], ice, departure_weights, weld_rate, cover)
+    out = back(grown, cover, rate)
     return out.reshape(ice_area.shape)
 
 

time: 32.1 us -> 30 us (0.935)
  the two profiles are of different devices: /device:TPU:24 before, /device:TPU:2 now
where the time goes in v1:
time: 30 us; the launch traced here: 29.9 us
  Pallas kernels  29.9 us (100%)
    pallas_call x1, Pallas kernels, front(): pl.pallas_call(front_kernel, name='front', out_shape=(pltpu.VMEM((CATS, R...  26.4 us
    pallas_call x1, Pallas kernels, back(): pl.pallas_call(back_kernel, name='back', out_shape=jax.ShapeDtypeStruct((...  3.48 us

profile of v1, /device:TPU:2, one launch (start us, length us, event | category | flops | bytes accessed | tf_op | source)
XLA Modules:
  0.0 29.9 jit_solution(13329629327989360670)
XLA Ops:
  0.0 0.0 copy-start
  0.0 26.4 %front.1 = (f32[60,32,1024]{2,1,0:T(8,128)S(1)}, f32[256,128]{1,0:T(8,128)S(1)}) custom-call(s32[1,128]{1,0:T(1,128)} %route_hbm.1, f32[25,128,256]{2,1,0:T(8,128)} %bitcast.7, f32[60,32,1024]{2,1,0:T(8,128)} %bitcast.6, s32[9,32,1024]{2,1,0:T(8,128)} %shares_hbm.1, f32[32,1024]{1,0:T(8,128)} %weld_hbm.1, s32[1,32]{1,0:T(1,128)} %bitcast.4), custom_call_target="tpu_custom_call" | custom-call | tf_op jit(solution)/shard_map/front/pallas_call | solution.py:486
  26.4 0.0 copy-done
  26.4 3.5 %back.1 = f32[60,32,1024]{2,1,0:T(8,128)} custom-call(f32[60,32,1024]{2,1,0:T(8,128)S(1)} %get-tuple-element.7.welded_ref, s32[1,32]{1,0:T(1,128)S(1)} %bitcast.5, f32[256,128]{1,0:T(8,128)S(1)} %get-tuple-element.8.rate_ref), custom_call_target="tpu_custom_call" | custom-call | tf_op jit(solution)/shard_map/back/pallas_call | solution.py:585
Async XLA Ops:
  0.0 26.4 %copy-start = (s32[32,1]{0,1:T(1,128)S(1)}, s32[32,1]{0,1:T(1,128)}, u32[]{:S(2)}) copy-start(s32[32,1]{0,1:T(1,128)} %param.9) | copy-start | bytes 388

commit v2 on v1

--- a/solution.py
+++ b/solution.py
@@ -36,22 +36,42 @@
     return jnp.sum(jnp.where(mine, listed, 0.0), axis=1, keepdims=True)
 
 
+def toeplitz(c, x):
+    size = len(x)
+    half = size // 2
+    odd = all(c.get(d, 0.0) == -c.get(-d, 0.0) for d in range(size))
+    if size % 2 or (odd and size <= 6):
+        result = []
+        for k in range(size):
+            total = None
+            for d in range(size):
+                below, above = k - d, k + d
+                if odd and d and below >= 0 and above < size:
+                    term = (x[below] - x[above]) * c[d]
+                    total = term if total is None else total + term
+                    continue
+                for j, scale in ((below, c.get(d, 0.0)), (above, c.get(-d, 0.0))):
+                    if 0 <= j < size and scale:
+                        term = x[j] * scale
+                        total = term if total is None else total + term
+                    if d == 0:
+                        break
+            result.append(total)
+        return result
+    low, high = x[:half], x[half:]
+    span = range(1 - half, half)
+    both = toeplitz({d: c.get(d, 0.0) for d in span}, [p + q for p, q in zip(low, high)])
+    down = toeplitz({d: c.get(d + half, 0.0) - c.get(d, 0.0) for d in span}, low)
+    up = toeplitz({d: c.get(d - half, 0.0) - c.get(d, 0.0) for d in span}, high)
+    return [p + q for p, q in zip(both, up)] + [p + q for p, q in zip(both, down)]
+
+
 def welded(area, weld):
     grown = [None] * NFSD
     lost = None
+    totals = toeplitz({d: (1.0 if d > 0 else -1.0) / (1.0 + abs(d)) for d in range(1 - NFSD, NFSD) if d}, area)
     for k in range(NFSD):
-        total = None
-        for d in range(1, NFSD):
-            below, above = k - d, k + d
-            if below >= 0 and above < NFSD:
-                term = (area[below] - area[above]) * (1.0 / (1.0 + d))
-            elif below >= 0:
-                term = area[below] * (1.0 / (1.0 + d))
-            elif above < NFSD:
-                term = area[above] * (-1.0 / (1.0 + d))
-            else:
-                continue
-            total = term if total is None else total + term
+        total = totals[k]
         rate = weld * area[k]
         value = area[k] + rate * total
         if k > 0:
@@ -295,7 +315,7 @@
 
     at_first = lane == 0
     at_last = lane == 127
-    batch = 6
+    batch = 10
 
     def stencil_group(g):
         def stencil(block, carry):

time: 30 us -> 29 us (0.967)
  Pallas kernels: 29.9 us -> 28.9 us
    pallas_call x1, Pallas kernels: 26.4 us -> 25.4 us  [front(): pl.pallas_call(front_kernel, name='front', out_shape=(pltpu.VMEM((CATS, R...]
where the time goes in v2:
time: 29 us; the launch traced here: 28.9 us
  Pallas kernels  28.9 us (100%)
    pallas_call x1, Pallas kernels, front(): pl.pallas_call(front_kernel, name='front', out_shape=(pltpu.VMEM((CATS, R...  25.4 us
    pallas_call x1, Pallas kernels, back(): pl.pallas_call(back_kernel, name='back', out_shape=jax.ShapeDtypeStruct((...  3.48 us

profile of v2, /device:TPU:2, one launch (start us, length us, event | category | flops | bytes accessed | tf_op | source)
XLA Modules:
  0.0 28.9 jit_solution(8211081557693602447)
XLA Ops:
  0.0 0.0 copy-start
  0.0 25.4 %front.1 = (f32[60,32,1024]{2,1,0:T(8,128)S(1)}, f32[256,128]{1,0:T(8,128)S(1)}) custom-call(s32[1,128]{1,0:T(1,128)} %route_hbm.1, f32[25,128,256]{2,1,0:T(8,128)} %bitcast.7, f32[60,32,1024]{2,1,0:T(8,128)} %bitcast.6, s32[9,32,1024]{2,1,0:T(8,128)} %shares_hbm.1, f32[32,1024]{1,0:T(8,128)} %weld_hbm.1, s32[1,32]{1,0:T(1,128)} %bitcast.4), custom_call_target="tpu_custom_call" | custom-call | tf_op jit(solution)/shard_map/front/pallas_call | solution.py:506
  25.4 0.0 copy-done
  25.4 3.5 %back.1 = f32[60,32,1024]{2,1,0:T(8,128)} custom-call(f32[60,32,1024]{2,1,0:T(8,128)S(1)} %get-tuple-element.7.welded_ref, s32[1,32]{1,0:T(1,128)S(1)} %bitcast.5, f32[256,128]{1,0:T(8,128)S(1)} %get-tuple-element.8.rate_ref), custom_call_target="tpu_custom_call" | custom-call | tf_op jit(solution)/shard_map/back/pallas_call | solution.py:605
Async XLA Ops:
  0.0 25.4 %copy-start = (s32[32,1]{0,1:T(1,128)S(1)}, s32[32,1]{0,1:T(1,128)}, u32[]{:S(2)}) copy-start(s32[32,1]{0,1:T(1,128)} %param.9) | copy-start | bytes 388

commit v3 on v2

--- a/solution.py
+++ b/solution.py
@@ -99,7 +99,7 @@
     inner_south = l > 0
     up = jnp.minimum(l + 1, NLAT - 1)
     down = jnp.maximum(l - 1, 0)
-    ahead = jnp.logical_or(b < NBLK // 2, l // 4 + lax.rem(l, 4) <= 3)
+    ahead = b < NBLK // 2
     behind = jnp.logical_not(ahead)
 
     parts = 4
@@ -564,16 +564,6 @@
 
 
 def back_kernel(welded_ref, cover_ref, rate_ref, out_hbm, out_v, crack_v, out_sem):
-    for g in range(GROUPS):
-        rows = pl.ds(8 * g, 8)
-        covered = covered_rows(cover_ref[...], g)
-        for j in range(TILES):
-            for half in range(2):
-                crack_v[pl.ds(8 * g + 4 * half, 4), pl.ds(128 * j, 128)] = rate_ref[
-                    pl.ds(16 * (j // 2) + 4 * g + 2 * half + j % 2, 4, stride=64), :
-                ]
-        crack_v[rows, :] = crack_v[rows, :] * covered * (0.1 / 11.0 / FREQ)
-
     def out_copy(part):
         group = part // NCAT
         cats = pl.ds(NFSD * (part - NCAT * group), NFSD)
@@ -594,9 +584,18 @@
         out_copy(part).start()
         return carry
 
-    parts = GROUPS * NCAT
-    lax.fori_loop(0, parts, chunk, 0)
-    for part in range(parts):
+    for g in range(GROUPS):
+        rows = pl.ds(8 * g, 8)
+        covered = covered_rows(cover_ref[...], g)
+        for j in range(TILES):
+            for half in range(2):
+                crack_v[pl.ds(8 * g + 4 * half, 4), pl.ds(128 * j, 128)] = rate_ref[
+                    pl.ds(16 * (j // 2) + 4 * g + 2 * half + j % 2, 4, stride=64), :
+                ]
+        crack_v[rows, :] = crack_v[rows, :] * covered * (0.1 / 11.0 / FREQ)
+        lax.fori_loop(g * NCAT, (g + 1) * NCAT, chunk, 0)
+
+    for part in range(GROUPS * NCAT):
         out_copy(part).wait()
 
 

time: 29 us -> 28.3 us (0.976)
  the two profiles are of different devices: /device:TPU:2 before, /device:TPU:7 now
where the time goes in v3:
time: 28.3 us; the launch traced here: 28.2 us
  Pallas kernels  28.2 us (100%)
    pallas_call x1, Pallas kernels, front(): pl.pallas_call(front_kernel, name='front', out_shape=(pltpu.VMEM((CATS, R...  24.8 us
    pallas_call x1, Pallas kernels, back(): pl.pallas_call(back_kernel, name='back', out_shape=jax.ShapeDtypeStruct((...  3.45 us

profile of v3, /device:TPU:7, one launch (start us, length us, event | category | flops | bytes accessed | tf_op | source)
XLA Modules:
  0.0 28.2 jit_solution(14196367357579822791)
XLA Ops:
  0.0 0.0 copy-start
  0.0 24.8 %front.1 = (f32[60,32,1024]{2,1,0:T(8,128)S(1)}, f32[256,128]{1,0:T(8,128)S(1)}) custom-call(s32[1,128]{1,0:T(1,128)} %route_hbm.1, f32[25,128,256]{2,1,0:T(8,128)} %bitcast.7, f32[60,32,1024]{2,1,0:T(8,128)} %bitcast.6, s32[9,32,1024]{2,1,0:T(8,128)} %shares_hbm.1, f32[32,1024]{1,0:T(8,128)} %weld_hbm.1, s32[1,32]{1,0:T(1,128)} %bitcast.4), custom_call_target="tpu_custom_call" | custom-call | tf_op jit(solution)/shard_map/front/pallas_call | solution.py:506
  24.8 0.0 copy-done
  24.8 3.4 %back.1 = f32[60,32,1024]{2,1,0:T(8,128)} custom-call(f32[60,32,1024]{2,1,0:T(8,128)S(1)} %get-tuple-element.7.welded_ref, s32[1,32]{1,0:T(1,128)S(1)} %bitcast.5, f32[256,128]{1,0:T(8,128)S(1)} %get-tuple-element.8.rate_ref), custom_call_target="tpu_custom_call" | custom-call | tf_op jit(solution)/shard_map/back/pallas_call | solution.py:604
Async XLA Ops:
  0.0 24.8 %copy-start = (s32[32,1]{0,1:T(1,128)S(1)}, s32[32,1]{0,1:T(1,128)}, u32[]{:S(2)}) copy-start(s32[32,1]{0,1:T(1,128)} %param.9) | copy-start | bytes 388
